TPU v7x, 32 devices: a whole 2x2x4 slice. The times are simulated.
32 devices in a mesh: groups: 2 (over x), tm: 4 (over y, core), tile: 4 (over z).
Axes of the slice: x: 2, y: 2, z: 4, core: 2. Of those that a mesh axis runs over, the one named last changes fastest.
Arguments:
- activations: float32 [24, 8, 64, 384], P(('groups', 'tm'), 'tile'), parts along dimension 0, may hold values from -200 to 200, as said below
- gain_attention: float32 [384], replicated, may hold values from 0.1 to 1.9
- w_query: float32 [384, 384], replicated, may hold values from -10 to 10, as said below
- w_key: float32 [384, 384], replicated, may hold values from -10 to 10, as said below
- w_value: float32 [384, 384], replicated, may hold values from -0.3125 to 0.3125
- w_out: float32 [384, 384], replicated, may hold values from -0.3125 to 0.3125
- gain_conv: float32 [384], replicated, may hold values from 0.1 to 1.9
- conv_weight: float32 [27, 384, 384], P(None, 'tm'), may hold values from -0.0625 to 0.0625
Outputs:
- attended: float32 [24, 8, 64, 384], P(('groups', 'tm'), 'tile'), parts along dimension 0
- conv_out: float32 [24, 8, 64, 384], P(('groups', 'tm'), 'tile'), parts along dimension 0
There are 2 independent parts, one for each index of `groups`. A program takes and returns all parts, laid end to end along the dimension named above; an argument that names none is the same for every part. Nothing has to cross between parts.
Inputs may be any that keep to these rules, and one draw needn't show every extreme that they name: `activations`: finite latent features. `w_query`: finite projection entries. `w_key`: finite projection entries.
All inputs are finite; a program needn't handle non-finite values.
Results may differ from a plain program's by a relative error of at most 0.00023.
Values sent between devices are 32-bit elements; how exact they have to be, the bound alone decides.
A program may use at most 128 MiB of HBM per device.

v0:
```python
import math
import jax
import jax.numpy as jnp
from jax import lax
from jax.sharding import PartitionSpec as P


def from_behind(block, axis, distance):
    devices = range(lax.axis_size(axis))
    route = [(i - distance, i) for i in devices if i - distance in devices]
    return lax.ppermute(block, axis, route)


def padded_2(x, sides, width):
    for axis, dim in sides:
        size, length = (lax.axis_size(axis), x.shape[dim])
        up = [(i, (i + 1) % size) for i in range(size - 1)]
        down = [(j, i) for i, j in up]
        last = lax.slice_in_dim(x, length - width, length, axis=dim)
        leading = lax.slice_in_dim(x, 0, width, axis=dim)
        before = lax.ppermute(last, axis, up)
        after = lax.ppermute(leading, axis, down)
        x = jnp.concatenate([before, x, after], axis=dim)
    return x


def rms_scale(values, gain):
    return values * lax.rsqrt(jnp.mean(values * values, axis=-1, keepdims=True) + 1e-06) * gain


def tap_columns(source, frame_count, row_count, width_cells):
    pieces = []
    for shift_t in range(3):
        for shift_y in range(3):
            for shift_x in range(3):
                pieces.append(
                    source[
                        ...,
                        shift_t : shift_t + frame_count,
                        shift_y : shift_y + row_count,
                        shift_x : shift_x + width_cells,
                        :,
                    ]
                )
    joined = jnp.concatenate(pieces, axis=-1)
    return joined.reshape(-1, joined.shape[-1])


def body(activations, gain_attention, w_query, w_key, w_value, w_out, gain_conv, conv_weight):
    highest = lax.Precision.HIGHEST
    frame_count, row_count, width_cells, channels = activations.shape
    tokens = row_count * width_cells
    pixels = frame_count * tokens
    scale = 1.0 / math.sqrt(channels)
    normed = rms_scale(activations, gain_attention).reshape(pixels, channels)
    queries = jnp.dot(normed, w_query, precision=highest).reshape(frame_count, tokens, channels)
    key_rows = jnp.dot(normed, w_key, precision=highest).reshape(frame_count, tokens, channels)
    values = jnp.dot(normed, w_value, precision=highest).reshape(frame_count, tokens, channels)
    running = jnp.full((frame_count, tokens), -1e30, jnp.float32)
    key_piece = lax.all_gather(key_rows, "tile", axis=1, tiled=True)
    value_piece = lax.all_gather(values, "tile", axis=1, tiled=True)
    scores = jnp.einsum("fqc,fkc->fqk", queries, key_piece, precision=highest) * scale
    largest = jnp.maximum(running, jnp.max(scores, axis=-1))
    powers = jnp.exp(scores - largest[..., None])
    summed = jnp.sum(powers, axis=-1)
    accumulated = jnp.einsum("fqk,fkc->fqc", powers, value_piece, precision=highest)
    running, summed, accumulated = (largest, summed, accumulated)
    mixed = accumulated / summed[..., None]
    attended = activations + jnp.dot(
        mixed.reshape(pixels, channels), w_out, precision=highest
    ).reshape(activations.shape)
    hidden = jax.nn.silu(rms_scale(attended, gain_conv))
    cached = from_behind(hidden[frame_count - 2 :], "tm", 1)
    stacked = jnp.concatenate([cached, hidden], axis=0)
    padded = padded_2(stacked, (("tile", 1),), 1)
    padded = jnp.pad(padded, ((0, 0), (0, 0), (1, 1), (0, 0)))
    piece = lax.all_gather(conv_weight, "tm", axis=1, tiled=True)
    count = piece.shape[1]
    columns = tap_columns(padded, frame_count, row_count, width_cells)
    conv_out = jnp.dot(columns, piece.reshape(27 * count, channels), precision=highest)
    return (attended, conv_out.reshape(activations.shape))


def solution(mesh):
    return jax.shard_map(
        body,
        mesh=mesh,
        in_specs=(
            P(("groups", "tm"), "tile", None, None),
            P(),
            P(),
            P(),
            P(),
            P(),
            P(),
            P(None, "tm", None),
        ),
        out_specs=(
            P(("groups", "tm"), "tile", None, None),
            P(("groups", "tm"), "tile", None, None),
        ),
        check_vma=False,
    )
```

profile of v0, /device:TPU:0, one launch (start us, length us, event | category | flops | bytes accessed | tf_op | source)
XLA Modules:
  0.0 256.4 jit_solution(7575440983940319005)
XLA Ops:
  7.2 1.3 multiply_reduce_fusion.1
  8.5 1.2 multiply_multiply_fusion
  9.7 3.1 %fusion.8 = f32[3,128,384]{2,1,0:T(8,128)} fusion(f32[3,128,384]{2,1,0:T(8,128)S(1)} %bitcast.33, f32[384,384]{1,0:T(8,128)} %param.11), kind=kOutput, calls=%fused_computation.50 | convolution fusion | flops 679477248 | bytes 1769472 | tf_op jit(solution)/shard_map/dot_general | solution.py:57
  13.0 3.1 %fusion.6 = f32[3,128,384]{2,1,0:T(8,128)} fusion(f32[3,128,384]{2,1,0:T(8,128)S(1)} %bitcast.34, f32[384,384]{1,0:T(8,128)} %param.12), kind=kOutput, calls=%fused_computation.48 | convolution fusion | flops 679477248 | bytes 1769472 | tf_op jit(solution)/shard_map/dot_general | solution.py:58
  16.9 2.3 fusion.10
  19.2 47.0 %all-gather.4.cloned.1.call-done = f32[3,512,384]{2,1,0:T(8,128)} async-done(((f32[3,128,384]{2,1,0:T(8,128)}), f32[3,512,384]{2,1,0:T(8,128)}) %all-gather.4.cloned.1.call-update) | async-done | bytes 2359312 | tf_op jit(solution)/shard_map/all_gather | solution.py:60
  66.2 4.3 %fusion.15 = (f32[3,128]{1,0:T(4,128)S(1)}, f32[3,128,512]{2,1,0:T(8,128)S(1)}) fusion(f32[3,128,384]{2,1,0:T(8,128)S(1)} %fusion.10, f32[3,512,384]{2,1,0:T(8,128)} %all-gather.4.cloned.1.call-done), kind=kOutput, calls=%fused_computation.65 | convolution fusion | flops 906362496 | bytes 3737088 | tf_op jit(solution)/shard_map/fqc,fkc->fqk/dot_general | solution.py:62
  70.8 46.9 %all-gather.6.cloned.1.call-done = f32[3,512,384]{2,1,0:T(8,128)} async-done(((f32[3,128,384]{2,1,0:T(8,128)}), f32[3,512,384]{2,1,0:T(8,128)}) %all-gather.6.cloned.1.call-update) | async-done | bytes 2359312 | tf_op jit(solution)/shard_map/all_gather | solution.py:61
  117.7 3.5 %convolution_divide_fusion = f32[3,128,384]{2,1,0:T(8,128)S(1)} fusion(f32[3,512,384]{2,1,0:T(8,128)} %all-gather.6.cloned.1.call-done, f32[3,128,512]{2,1,0:T(8,128)S(1)} %get-tuple-element.7, f32[3,128]{1,0:T(4,128)S(1)} %broadcast_maximum_fusion, f32[3,128]{1,0:T(4,128)S(1)} %fusion.1), kind=kOutput, calls=%fused_computation.16 | convolution fusion | flops 906313728 | bytes 3738624 | tf_op jit(solution)/shard_map/fqk,fkc->fqc/dot_general | solution.py:66
  121.2 1.4 multiply_reduce_fusion
  122.9 1.8 collective-permute-start
  124.7 1.3 collective-permute-done
  126.1 1.6 collective-permute-start.1
  127.7 1.5 collective-permute-start.2
  129.2 4.8 %collective-permute-done.1 = f32[5,1,64,384]{3,2,1,0:T(8,128)S(1)} collective-permute-done((f32[5,1,64,384]{3,2,1,0:T(8,128)S(1)}, f32[5,1,64,384]{3,2,1,0:T(8,128)S(1)}, u32[]{:S(2)}, u32[]{:S(2)}) %collective-permute-start.1) | collective-permute-done | bytes 491552 | tf_op jit(solution)/shard_map/ppermute | solution.py:21
  134.0 4.5 %collective-permute-done.2 = f32[5,1,64,384]{3,2,1,0:T(8,128)S(1)} collective-permute-done((f32[5,1,64,384]{3,2,1,0:T(8,128)S(1)}, f32[5,1,64,384]{3,2,1,0:T(8,128)S(1)}, u32[]{:S(2)}, u32[]{:S(2)}) %collective-permute-start.2) | collective-permute-done | bytes 491552 | tf_op jit(solution)/shard_map/ppermute | solution.py:22
  142.8 0.9 fusion.3
  143.7 1.0 slice_dynamic-update-slice_fusion.19
  154.7 0.9 slice_dynamic-update-slice_fusion.8
  156.5 0.9 slice_dynamic-update-slice_fusion.6
  159.2 1.1 constant_dynamic-update-slice_fusion
  161.3 1.0 slice_dynamic-update-slice_fusion.2
  164.0 55.2 %all-gather.8.cloned.1.call-done = f32[27,384,384]{2,1,0:T(8,128)} async-done(((f32[27,96,384]{2,1,0:T(8,128)}), f32[27,384,384]{2,1,0:T(8,128)}) %all-gather.8.cloned.1.call-update) | async-done | bytes 15925264 | tf_op jit(solution)/shard_map/all_gather | solution.py:77
  219.2 30.7 %fusion.16 = f32[3,2,64,384]{3,2,1,0:T(8,128)} fusion(f32[3,2,64,10368]{3,2,1,0:T(8,128)} %slice_dynamic-update-slice_fusion, f32[10368,384,1,1]{1,0,3,2:T(8,128)} %bitcast.32), kind=kOutput, calls=%fused_computation.66 | convolution fusion | flops 18345885696 | bytes 32440320 | tf_op jit(solution)/shard_map/dot_general | solution.py:80
  (44 shorter events, 21.1 us)
Async XLA Ops:
  7.2 114.0 %copy-start = (f32[384,384]{1,0:T(8,128)S(1)}, f32[384,384]{1,0:T(8,128)}, u32[]{:S(2)}) copy-start(f32[384,384]{1,0:T(8,128)} %param.13) | copy-start | bytes 1769476
  7.2 114.0 %copy-start.1 = (f32[3,2,64,384]{3,2,1,0:T(8,128)S(1)}, f32[3,2,64,384]{3,2,1,0:T(8,128)}, u32[]{:S(2)}) copy-start(f32[3,2,64,384]{3,2,1,0:T(8,128)} %param.8) | copy-start | bytes 1769476
  7.2 115.5 %copy-start.3 = (f32[384]{0:T(512)S(1)}, f32[384]{0:T(512)}, u32[]{:S(2)}) copy-start(f32[384]{0:T(512)} %param.14) | copy-start | bytes 4612
  7.2 59.0 %all-gather.4.cloned.1.call-start = ((), (), s32[]{:S(2)}) async-start(), calls=%async_computation | async-start | bytes 2949120 | tf_op jit(solution)/shard_map/all_gather | solution.py:60
  12.9 104.8 %all-gather.6.cloned.1.call-start = ((), (), s32[]{:S(2)}) async-start(), calls=%async_computation.1 | async-start | bytes 2949120 | tf_op jit(solution)/shard_map/all_gather | solution.py:61
  16.1 203.1 %all-gather.8.cloned.1.call-start = ((), (), s32[]{:S(2)}) async-start(), calls=%async_computation.2 | async-start | bytes 19906560 | tf_op jit(solution)/shard_map/all_gather | solution.py:77
  122.6 36.6 %copy-start.2 = (f32[3,2,64,384]{3,2,1,0:T(8,128)}, f32[3,2,64,384]{3,2,1,0:T(8,128)S(1)}, u32[]{:S(2)}) copy-start(f32[3,2,64,384]{3,2,1,0:T(8,128)S(1)} %get-tuple-element.9) | copy-start | bytes 1769476
  122.9 3.1 %collective-permute-start = (f32[2,2,64,384]{3,2,1,0:T(8,128)S(1)}, f32[2,2,64,384]{3,2,1,0:T(8,128)S(1)}, u32[]{:S(2)}, u32[]{:S(2)}) collective-permute-start(f32[2,2,64,384]{3,2,1,0:T(8,128)S(1)} %slice.135), channel_id=1, source_target_pairs={{0,4},{4,8},{8,12},{1,5},{5,9},{9,13},{2,6},{6,10},{10,14},{3,7},{... | collective-permute-start | bytes 1179656 | tf_op jit(solution)/shard_map/ppermute | solution.py:11
  126.1 8.0 %collective-permute-start.1 = (f32[5,1,64,384]{3,2,1,0:T(8,128)S(1)}, f32[5,1,64,384]{3,2,1,0:T(8,128)S(1)}, u32[]{:S(2)}, u32[]{:S(2)}) collective-permute-start(f32[5,1,64,384]{3,2,1,0:T(8,128)S(1)} %get-tuple-element.4), channel_id=1, source_target_pairs={{0,1},{1,2},{2,3},{4,5},{5,6},{6,7},{8,9},{9,10},{10,11},{12,13},{... | collective-permute-start | bytes 1474568 | tf_op jit(solution)/shard_map/ppermute | solution.py:21
  127.7 10.8 %collective-permute-start.2 = (f32[5,1,64,384]{3,2,1,0:T(8,128)S(1)}, f32[5,1,64,384]{3,2,1,0:T(8,128)S(1)}, u32[]{:S(2)}, u32[]{:S(2)}) collective-permute-start(f32[5,1,64,384]{3,2,1,0:T(8,128)S(1)} %get-tuple-element.5), channel_id=1, source_target_pairs={{1,0},{2,1},{3,2},{5,4},{6,5},{7,6},{9,8},{10,9},{11,10},{13,12},{... | collective-permute-start | bytes 1474568 | tf_op jit(solution)/shard_map/ppermute | solution.py:22
Sparse Core Ops, SparseCore 0:
  13.0 53.1 all-gather.3
  68.3 49.2 all-gather.5
  119.2 99.9 all-gather.7
where the time goes:
time: 257 us; the launch traced here: 256 us
  waiting for transfers between devices  160 us (62%)
  matrix products  48.5 us (19%)
  local copies, waits for them, and re-layouts  22 us (9%)
  between operations  13.9 us (5%)
  other arithmetic  6.63 us (3%)
  starting transfers between devices  5 us (2%)
    all_gather x1, waiting for transfers between devices, body(): piece = lax.all_gather(conv_weight, 'tm', axis=1, tiled=True)  55.2 us
    all_gather x1, waiting for transfers between devices, body(): key_piece = lax.all_gather(key_rows, 'tile', axis=1, tiled=True)  47 us
    all_gather x1, waiting for transfers between devices, body(): value_piece = lax.all_gather(values, 'tile', axis=1, tiled=True)  46.9 us
    dot_general x1, matrix products, body(): jnp.dot(columns, piece.reshape(27 * count, channels), precision=highest)  30.7 us
    unnamed x31, local copies, waits for them, and re-layouts  21 us
  transfers between devices with their start and end apart: 6, of which 6 were waited for; matrix products, arithmetic and copies ran while one was open for 16% of the time, Pallas kernels for 0%

commit v1 on v0

--- a/solution.py
+++ b/solution.py
@@ -58,7 +58,24 @@
     values = jnp.dot(normed, w_value, precision=highest).reshape(frame_count, tokens, channels)
     running = jnp.full((frame_count, tokens), -1e30, jnp.float32)
     key_piece = lax.all_gather(key_rows, "tile", axis=1, tiled=True)
-    value_piece = lax.all_gather(values, "tile", axis=1, tiled=True)
+    ways, here, step = (lax.axis_size("tile"), lax.axis_index("tile"), values.shape[1])
+    lengths = [n * ways if d == 1 else n for d, n in enumerate(values.shape)]
+    value_piece = lax.dynamic_update_slice_in_dim(
+        jnp.zeros(lengths, values.dtype), values, here * step, axis=1
+    )
+    going_up = going_down = values
+    for far in range(1, ways // 2 + 1):
+        going_up = lax.ppermute(going_up, "tile", [(d, (d + 1) % ways) for d in range(ways)])
+        value_piece = lax.dynamic_update_slice_in_dim(
+            value_piece, going_up, (here - far) % ways * step, axis=1
+        )
+        if 2 * far < ways:
+            going_down = lax.ppermute(
+                going_down, "tile", [(d, (d - 1) % ways) for d in range(ways)]
+            )
+            value_piece = lax.dynamic_update_slice_in_dim(
+                value_piece, going_down, (here + far) % ways * step, axis=1
+            )
     scores = jnp.einsum("fqc,fkc->fqk", queries, key_piece, precision=highest) * scale
     largest = jnp.maximum(running, jnp.max(scores, axis=-1))
     powers = jnp.exp(scores - largest[..., None])

time: 257 us -> 239 us (0.930)
  waiting for transfers between devices: 160 us -> 113 us
  starting transfers between devices: 5 us -> 29.6 us
  local copies, waits for them, and re-layouts: 22 us -> 25.4 us
    all_gather x1 -> x0, waiting for transfers between devices: 46.9 us -> none  [body(): value_piece = lax.all_gather(values, 'tile', axis=1, tiled=True)]
    ppermute x0 -> x3, waiting for transfers between devices: none -> 46.6 us  [the longest x2 36.7 us: body(): lax.ppermute(going_up, 'tile', [(d, (d + 1) % ways) for d in range(ways)])]
    all_gather x1, waiting for transfers between devices: 47 us -> 4.59 us  [body(): key_piece = lax.all_gather(key_rows, 'tile', axis=1, tiled=True)]
    ppermute x0 -> x3, starting transfers between devices: none -> 24.5 us  [the longest x2 22.5 us: body(): lax.ppermute(going_up, 'tile', [(d, (d + 1) % ways) for d in range(ways)])]
    all_gather x1, waiting for transfers between devices: 55.2 us -> 50.3 us  [body(): piece = lax.all_gather(conv_weight, 'tm', axis=1, tiled=True)]
    dynamic_update_slice x0 -> x3, local copies, waits for them, and re-layouts: none -> 3.31 us  [the longest x2 2.21 us: body(): lax.dynamic_update_slice_in_dim(value_piece, going_up, (here - far) % way...]
    unnamed x31 -> x29, local copies, waits for them, and re-layouts: 21 us -> 21 us
  transfers between devices with their start and end apart: 6 -> 8, of which waited for: 6 -> 8; matrix products, arithmetic and copies ran while one was open for 16% -> 19% of each run, Pallas kernels for 0% -> 0%
where the time goes in v1:
time: 239 us; the launch traced here: 237 us
  waiting for transfers between devices  113 us (47%)
  matrix products  48.2 us (20%)
  starting transfers between devices  29.6 us (12%)
  local copies, waits for them, and re-layouts  25.4 us (11%)
  between operations  14.2 us (6%)
  other arithmetic  6.52 us (3%)
    all_gather x1, waiting for transfers between devices, body(): piece = lax.all_gather(conv_weight, 'tm', axis=1, tiled=True)  50.3 us
    ppermute x2, waiting for transfers between devices, body(): lax.ppermute(going_up, 'tile', [(d, (d + 1) % ways) for d in range(ways)])  36.7 us
    dot_general x1, matrix products, body(): jnp.dot(columns, piece.reshape(27 * count, channels), precision=highest)  30.7 us
    ppermute x2, starting transfers between devices, body(): lax.ppermute(going_up, 'tile', [(d, (d + 1) % ways) for d in range(ways)])  22.5 us
    unnamed x29, local copies, waits for them, and re-layouts  21 us
    ppermute x1, waiting for transfers between devices, body(): lax.ppermute(going_down, 'tile', [(d, (d - 1) % ways) for d in range(ways)])  9.86 us
    ppermute x1, waiting for transfers between devices, padded_2(): before = lax.ppermute(last, axis, up)  4.82 us
  transfers between devices with their start and end apart: 8, of which 8 were waited for; matrix products, arithmetic and copies ran while one was open for 19% of the time, Pallas kernels for 0%

profile of v1, /device:TPU:0, one launch (start us, length us, event | category | flops | bytes accessed | tf_op | source)
XLA Modules:
  0.0 236.6 jit_solution(10954295819229510925)
XLA Ops:
  7.2 1.2 multiply_reduce_fusion.1
  8.5 1.2 multiply_multiply_fusion
  9.7 3.1 %fusion.8 = f32[3,128,384]{2,1,0:T(8,128)} fusion(f32[3,128,384]{2,1,0:T(8,128)S(1)} %bitcast.35, f32[384,384]{1,0:T(8,128)} %param.11), kind=kOutput, calls=%fused_computation.50 | convolution fusion | flops 679477248 | bytes 1769472 | tf_op jit(solution)/shard_map/dot_general | solution.py:57
  13.8 2.1 constant_dynamic-update-slice_fusion.4
  15.9 3.0 %collective-permute-start = (f32[3,128,384]{2,1,0:T(8,128)}, f32[3,128,384]{2,1,0:T(8,128)}, u32[]{:S(2)}, u32[]{:S(2)}) collective-permute-start(f32[3,128,384]{2,1,0:T(8,128)} %get-tuple-element.7), channel_id=1, source_target_pairs={{0,1},{1,2},{2,3},{3,0},{4,5},{5,6},{6,7},{7,4},{8,9},{9,10},{10,1... | collective-permute-start | bytes 1769480 | tf_op jit(solution)/shard_map/ppermute | solution.py:68
  18.9 2.0 collective-permute-start.1
  20.9 21.7 %collective-permute-done = f32[3,128,384]{2,1,0:T(8,128)} collective-permute-done((f32[3,128,384]{2,1,0:T(8,128)}, f32[3,128,384]{2,1,0:T(8,128)}, u32[]{:S(2)}, u32[]{:S(2)}) %collective-permute-start) | collective-permute-done | bytes 589856 | tf_op jit(solution)/shard_map/ppermute | solution.py:68
  42.6 19.5 %collective-permute-start.2 = (f32[3,128,384]{2,1,0:T(8,128)}, f32[3,128,384]{2,1,0:T(8,128)}, u32[]{:S(2)}, u32[]{:S(2)}) collective-permute-start(f32[3,128,384]{2,1,0:T(8,128)} %collective-permute-done), channel_id=1, source_target_pairs={{0,1},{1,2},{2,3},{3,0},{4,5},{5,6},{6,7},{7,4},{8,9},{9,10},{10,1... | collective-permute-start | bytes 1769480 | tf_op jit(solution)/shard_map/ppermute | solution.py:68
  62.1 3.1 %fusion.10 = f32[3,128,384]{2,1,0:T(8,128)} fusion(f32[3,128,384]{2,1,0:T(8,128)S(1)} %bitcast.37, f32[384,384]{1,0:T(8,128)} %param.10), kind=kOutput, calls=%fused_computation.52 | convolution fusion | flops 679477248 | bytes 1769472 | tf_op jit(solution)/shard_map/dot_general | solution.py:56
  66.4 9.9 %collective-permute-done.1 = f32[3,128,384]{2,1,0:T(8,128)} collective-permute-done((f32[3,128,384]{2,1,0:T(8,128)}, f32[3,128,384]{2,1,0:T(8,128)}, u32[]{:S(2)}, u32[]{:S(2)}) %collective-permute-start.1) | collective-permute-done | bytes 589856 | tf_op jit(solution)/shard_map/ppermute | solution.py:73
  77.3 15.0 %collective-permute-done.2 = f32[3,128,384]{2,1,0:T(8,128)} collective-permute-done((f32[3,128,384]{2,1,0:T(8,128)}, f32[3,128,384]{2,1,0:T(8,128)}, u32[]{:S(2)}, u32[]{:S(2)}) %collective-permute-start.2) | collective-permute-done | bytes 589856 | tf_op jit(solution)/shard_map/ppermute | solution.py:68
  93.5 4.6 %all-gather.3.cloned.1.call-done = f32[3,512,384]{2,1,0:T(8,128)} async-done(((f32[3,128,384]{2,1,0:T(8,128)}), f32[3,512,384]{2,1,0:T(8,128)}) %all-gather.3.cloned.1.call-update) | async-done | bytes 2359312 | tf_op jit(solution)/shard_map/all_gather | solution.py:60
  98.0 4.4 %fusion.15 = (f32[3,128]{1,0:T(4,128)S(1)}, f32[3,128,512]{2,1,0:T(8,128)S(1)}) fusion(f32[3,128,384]{2,1,0:T(8,128)} %fusion.10, f32[3,512,384]{2,1,0:T(8,128)} %all-gather.3.cloned.1.call-done), kind=kOutput, calls=%fused_computation.69 | convolution fusion | flops 906362496 | bytes 3737088 | tf_op jit(solution)/shard_map/fqc,fkc->fqk/dot_general | solution.py:79
  102.8 1.9 convolution_divide_fusion
  104.7 2.8 %multiply_reduce_fusion = (f32[3,2,64]{2,1,0:T(2,128)S(1)}, f32[3,2,64,384]{3,2,1,0:T(8,128)S(1)}) fusion(f32[3,2,64,384]{3,2,1,0:T(8,128)} %param.8, f32[3,2,64,384]{3,2,1,0:T(8,128)S(1)} %bitcast.38, f32[384,384]{1,0:T(8,128)} %param.13), kind=kOutput, calls=%fused_computation.55 | convolution fusion | flops 679919232 | bytes 2360832 | tf_op jit(solution)/shard_map/dot_general | solution.py:86
  107.8 2.0 collective-permute-start.3
  109.8 1.3 collective-permute-done.3
  111.2 1.5 collective-permute-start.4
  112.7 1.5 collective-permute-start.5
  114.2 4.8 %collective-permute-done.4 = f32[5,1,64,384]{3,2,1,0:T(8,128)S(1)} collective-permute-done((f32[5,1,64,384]{3,2,1,0:T(8,128)S(1)}, f32[5,1,64,384]{3,2,1,0:T(8,128)S(1)}, u32[]{:S(2)}, u32[]{:S(2)}) %collective-permute-start.4) | collective-permute-done | bytes 491552 | tf_op jit(solution)/shard_map/ppermute | solution.py:21
  119.0 4.4 %collective-permute-done.5 = f32[5,1,64,384]{3,2,1,0:T(8,128)S(1)} collective-permute-done((f32[5,1,64,384]{3,2,1,0:T(8,128)S(1)}, f32[5,1,64,384]{3,2,1,0:T(8,128)S(1)}, u32[]{:S(2)}, u32[]{:S(2)}) %collective-permute-start.5) | collective-permute-done | bytes 491552 | tf_op jit(solution)/shard_map/ppermute | solution.py:22
  144.0 1.1 constant_dynamic-update-slice_fusion
  148.8 50.3 %all-gather.5.cloned.1.call-done = f32[27,384,384]{2,1,0:T(8,128)} async-done(((f32[27,96,384]{2,1,0:T(8,128)}), f32[27,384,384]{2,1,0:T(8,128)}) %all-gather.5.cloned.1.call-update) | async-done | bytes 15925264 | tf_op jit(solution)/shard_map/all_gather | solution.py:94
  199.1 30.7 %fusion.16 = f32[3,2,64,384]{3,2,1,0:T(8,128)} fusion(f32[3,2,64,10368]{3,2,1,0:T(8,128)} %slice_dynamic-update-slice_fusion, f32[10368,384,1,1]{1,0,3,2:T(8,128)} %bitcast.34), kind=kOutput, calls=%fused_computation.70 | convolution fusion | flops 18345885696 | bytes 32440320 | tf_op jit(solution)/shard_map/dot_general | solution.py:97
  (49 shorter events, 29.2 us)
Async XLA Ops:
  7.2 6.6 %copy-start = (f32[384,384]{1,0:T(8,128)S(1)}, f32[384,384]{1,0:T(8,128)}, u32[]{:S(2)}) copy-start(f32[384,384]{1,0:T(8,128)} %param.12) | copy-start | bytes 1769476
  7.2 100.4 %copy-start.2 = (f32[384]{0:T(512)S(1)}, f32[384]{0:T(512)}, u32[]{:S(2)}) copy-start(f32[384]{0:T(512)} %param.14) | copy-start | bytes 4612
  7.2 90.9 %all-gather.3.cloned.1.call-start = ((), (), s32[]{:S(2)}) async-start(), calls=%async_computation | async-start | bytes 2949120 | tf_op jit(solution)/shard_map/all_gather | solution.py:60
  12.9 186.2 %all-gather.5.cloned.1.call-start = ((), (), s32[]{:S(2)}) async-start(), calls=%async_computation.1 | async-start | bytes 19906560 | tf_op jit(solution)/shard_map/all_gather | solution.py:94
  15.9 26.7 %collective-permute-start = (f32[3,128,384]{2,1,0:T(8,128)}, f32[3,128,384]{2,1,0:T(8,128)}, u32[]{:S(2)}, u32[]{:S(2)}) collective-permute-start(f32[3,128,384]{2,1,0:T(8,128)} %get-tuple-element.7), channel_id=1, source_target_pairs={{0,1},{1,2},{2,3},{3,0},{4,5},{5,6},{6,7},{7,4},{8,9},{9,10},{10,1... | collective-permute-start | bytes 1769480 | tf_op jit(solution)/shard_map/ppermute | solution.py:68
  18.9 57.3 %collective-permute-start.1 = (f32[3,128,384]{2,1,0:T(8,128)}, f32[3,128,384]{2,1,0:T(8,128)}, u32[]{:S(2)}, u32[]{:S(2)}) collective-permute-start(f32[3,128,384]{2,1,0:T(8,128)} %get-tuple-element.7), channel_id=1, source_target_pairs={{0,3},{1,0},{2,1},{3,2},{4,7},{5,4},{6,5},{7,6},{8,11},{9,8},{10,9... | collective-permute-start | bytes 1769480 | tf_op jit(solution)/shard_map/ppermute | solution.py:73
  42.6 49.7 %collective-permute-start.2 = (f32[3,128,384]{2,1,0:T(8,128)}, f32[3,128,384]{2,1,0:T(8,128)}, u32[]{:S(2)}, u32[]{:S(2)}) collective-permute-start(f32[3,128,384]{2,1,0:T(8,128)} %collective-permute-done), channel_id=1, source_target_pairs={{0,1},{1,2},{2,3},{3,0},{4,5},{5,6},{6,7},{7,4},{8,9},{9,10},{10,1... | collective-permute-start | bytes 1769480 | tf_op jit(solution)/shard_map/ppermute | solution.py:68
  107.5 36.5 %copy-start.1 = (f32[3,2,64,384]{3,2,1,0:T(8,128)}, f32[3,2,64,384]{3,2,1,0:T(8,128)S(1)}, u32[]{:S(2)}) copy-start(f32[3,2,64,384]{3,2,1,0:T(8,128)S(1)} %get-tuple-element.11) | copy-start | bytes 1769476
  107.8 3.3 %collective-permute-start.3 = (f32[2,2,64,384]{3,2,1,0:T(8,128)S(1)}, f32[2,2,64,384]{3,2,1,0:T(8,128)S(1)}, u32[]{:S(2)}, u32[]{:S(2)}) collective-permute-start(f32[2,2,64,384]{3,2,1,0:T(8,128)S(1)} %slice.135), channel_id=1, source_target_pairs={{0,4},{4,8},{8,12},{1,5},{5,9},{9,13},{2,6},{6,10},{10,14},{3,7},{... | collective-permute-start | bytes 1179656 | tf_op jit(solution)/shard_map/ppermute | solution.py:11
  111.2 7.8 %collective-permute-start.4 = (f32[5,1,64,384]{3,2,1,0:T(8,128)S(1)}, f32[5,1,64,384]{3,2,1,0:T(8,128)S(1)}, u32[]{:S(2)}, u32[]{:S(2)}) collective-permute-start(f32[5,1,64,384]{3,2,1,0:T(8,128)S(1)} %get-tuple-element.4), channel_id=1, source_target_pairs={{0,1},{1,2},{2,3},{4,5},{5,6},{6,7},{8,9},{9,10},{10,11},{12,13},{... | collective-permute-start | bytes 1474568 | tf_op jit(solution)/shard_map/ppermute | solution.py:21
  112.7 10.7 %collective-permute-start.5 = (f32[5,1,64,384]{3,2,1,0:T(8,128)S(1)}, f32[5,1,64,384]{3,2,1,0:T(8,128)S(1)}, u32[]{:S(2)}, u32[]{:S(2)}) collective-permute-start(f32[5,1,64,384]{3,2,1,0:T(8,128)S(1)} %get-tuple-element.5), channel_id=1, source_target_pairs={{1,0},{2,1},{3,2},{5,4},{6,5},{7,6},{9,8},{10,9},{11,10},{13,12},{... | collective-permute-start | bytes 1474568 | tf_op jit(solution)/shard_map/ppermute | solution.py:22
Sparse Core Ops, SparseCore 0:
  13.0 85.0 all-gather.2
  99.6 99.4 all-gather.4
